TPU v7x, 256 devices: a whole 4x4x8 slice. The times are simulated.
256 devices in a mesh: dp: 32 (over x, z), frame: 8 (over y, core).
Axes of the slice: x: 4, y: 4, z: 8, core: 2. Of those that a mesh axis runs over, the one named last changes fastest.
Arguments:
- features: bfloat16 [32, 16, 32, 64, 128], P('dp', 'frame'), may hold values from -6 to 6
- vis_block: int32 [32, 16, 16, 2], P('dp', None, 'frame'), may hold values from 0 to 31
- vis_count: int32 [32, 16, 16], P('dp', None, 'frame'), may hold values from 1 to 2
- query_frame: int32 [32, 256], P('dp'), may hold values from 0 to 15
- query_block: int32 [32, 256], P('dp'), may hold values from 0 to 31
- query_cell: int32 [32, 256], P('dp'), may hold values from 0 to 63
- cotangent: bfloat16 [32, 4, 256, 16], P('dp', None, 'frame')
- w_in: bfloat16 [128, 384], replicated, may hold values from -0.5 to 0.5
- gain: float32 [384], replicated, may hold values from 0.1 to 1.9
- w_qkv: bfloat16 [384, 1152], replicated, may hold values from -0.3125 to 0.3125
- w_out: bfloat16 [384, 384], replicated, may hold values from -0.3125 to 0.3125
- w_head: bfloat16 [4, 384], replicated, may hold values from -0.3125 to 0.3125
Outputs:
- grad_in: float32 [128, 384], replicated
- grad_gain: float32 [384], replicated
- grad_qkv: float32 [384, 1152], replicated
- grad_out: float32 [384, 384], replicated
- grad_head: float32 [4, 384], replicated
Inputs may be any that keep to these rules, and one draw needn't show every extreme that they name: vis_count counts the leading visible slots of vis_block.
All inputs are finite; a program needn't handle non-finite values.
Results may differ from a plain program's by a relative error of at most 0.012.
Values may be sent and summed in bfloat16 or wider, within the bound.
No kernel may reach another device: no remote copies, remote signals or barrier semaphores. Data moves between devices by JAX's collectives and lax.ppermute only.
A program may use at most 64 MiB of HBM per device.

v0:
```python
import jax
import jax.numpy as jnp
from jax import lax
from jax.sharding import PartitionSpec as P

HEADS = 8


def attend(query, keys, values):
    scale = query.shape[-1] ** (-0.5)
    scores = (
        jnp.einsum("nfhd,nghd->nhfg", query.astype(jnp.float32), keys.astype(jnp.float32)) * scale
    )
    probs = jax.nn.softmax(scores, axis=-1).astype(jnp.bfloat16)
    probs = lax.optimization_barrier(probs)
    mixed = jnp.einsum("nhfg,nghd->nfhd", probs.astype(jnp.float32), values.astype(jnp.float32))
    return mixed.astype(jnp.bfloat16)


def inner_rows(left, right):
    return lax.dot_general(
        left, right, (((0,), (0,)), ((), ())), preferred_element_type=jnp.float32
    )


def outer_cols(left, right):
    return lax.dot_general(
        left, right, (((1,), (1,)), ((), ())), preferred_element_type=jnp.float32
    )


def local_grads(corr, cot, w_in, gain, w_qkv, w_out, w_head):
    tracks, frames, width = corr.shape
    total = tracks * frames
    hid = w_in.shape[1]
    head_size = hid // HEADS
    rows = corr.reshape(total, width)
    x_zero = jnp.dot(rows, w_in, preferred_element_type=jnp.float32)
    centred = x_zero - jnp.mean(x_zero, axis=-1, keepdims=True)
    inv_std = lax.rsqrt(jnp.mean(centred * centred, axis=-1, keepdims=True) + 1e-05)
    normed = centred * inv_std
    hidden = (normed * gain).astype(jnp.bfloat16)
    qkv = jnp.dot(hidden, w_qkv, preferred_element_type=jnp.float32).astype(jnp.bfloat16)
    split = qkv.reshape(tracks, frames, 3, HEADS, head_size)
    mixed, backward = jax.vjp(attend, split[:, :, 0], split[:, :, 1], split[:, :, 2])
    mixed = mixed.reshape(total, hid)
    y_out = (x_zero + jnp.dot(mixed, w_out, preferred_element_type=jnp.float32)).astype(
        jnp.bfloat16
    )
    ct_rows = cot.reshape(cot.shape[0], total)
    g_head = jnp.dot(ct_rows, y_out, preferred_element_type=jnp.float32)
    d_y = inner_rows(ct_rows, w_head)
    d_y16 = d_y.astype(jnp.bfloat16)
    g_out = inner_rows(mixed, d_y16)
    d_mixed = outer_cols(d_y16, w_out).astype(jnp.bfloat16)
    d_q, d_k, d_v = backward(d_mixed.reshape(tracks, frames, HEADS, head_size))
    d_qkv = jnp.stack([d_q, d_k, d_v], axis=2).reshape(total, 3 * hid)
    g_qkv = inner_rows(hidden, d_qkv)
    d_hidden = outer_cols(d_qkv, w_qkv)
    g_gain = jnp.sum(d_hidden * normed, axis=0)
    d_norm = d_hidden * gain
    d_x = (
        inv_std
        * (
            d_norm
            - jnp.mean(d_norm, axis=-1, keepdims=True)
            - normed * jnp.mean(d_norm * normed, axis=-1, keepdims=True)
        )
        + d_y
    )
    d_x16 = d_x.astype(jnp.bfloat16)
    g_in = inner_rows(rows, d_x16)
    return (g_in, g_gain, g_qkv, g_out, g_head)


def body(
    features,
    vis_block,
    vis_count,
    query_frame,
    query_block,
    query_cell,
    cotangent,
    w_in,
    gain,
    w_qkv,
    w_out,
    w_head,
):
    feats = features[0]
    fr_dev = feats.shape[0]
    cells = feats.shape[2]
    width = feats.shape[3]
    trk_dev = cotangent.shape[2]
    frame_pos = lax.axis_index("frame")
    frames_q = query_frame[0]
    blocks_q = query_block[0]
    cells_q = query_cell[0]
    local = frames_q - frame_pos * fr_dev
    inside = (local >= 0) & (local < fr_dev)
    picked = feats[jnp.clip(local, 0, fr_dev - 1), blocks_q, cells_q].astype(jnp.float32)
    query = lax.psum_scatter(
        jnp.where(inside[:, None], picked, 0.0).astype(jnp.bfloat16),
        "frame",
        scatter_dimension=0,
        tiled=True,
    )
    groups = vis_block.shape[1]
    slots = vis_block.shape[3]
    frame_ids = jnp.arange(fr_dev, dtype=jnp.int32)[None, :, None]
    patches = feats[frame_ids, vis_block[0]]
    live = jnp.arange(slots, dtype=jnp.int32)[None, None, :] < vis_count[0][:, :, None]
    patches = jnp.where(live[..., None, None], patches, jnp.zeros((), jnp.bfloat16))
    scale = width ** (-0.5)
    outgoing = patches.reshape(groups, fr_dev, slots, cells * width)
    arrived = lax.all_to_all(outgoing, "frame", split_axis=0, concat_axis=1, tiled=True)
    own_groups = arrived.shape[0]
    all_frames = arrived.shape[1]
    arrived = arrived.reshape(own_groups, all_frames, slots, cells, width)
    corr = jnp.einsum(
        "gtc,gfkpc->gtfkp",
        query.reshape(own_groups, -1, width),
        arrived,
        preferred_element_type=jnp.float32,
    )
    corr = (corr * scale).astype(jnp.bfloat16).reshape(trk_dev, all_frames, slots * cells)
    g_in, g_gain, g_qkv, g_out, g_head = local_grads(
        corr, cotangent[0], w_in, gain, w_qkv, w_out, w_head
    )
    s_in, s_gain, s_qkv, s_out, s_head = lax.psum(
        (g_in, g_gain, g_qkv, g_out, g_head), ("dp", "frame")
    )
    return (s_in, s_gain, s_qkv, s_out, s_head)


def solution(mesh):
    in_specs = (
        P("dp", "frame", None, None, None),
        P("dp", None, "frame", None),
        P("dp", None, "frame"),
        P("dp", None),
        P("dp", None),
        P("dp", None),
        P("dp", None, "frame", None),
        P(),
        P(),
        P(),
        P(),
        P(),
    )
    out_specs = (P(), P(), P(), P(), P())
    return jax.shard_map(body, mesh=mesh, in_specs=in_specs, out_specs=out_specs, check_vma=False)
```

profile of v0, /device:TPU:2, one launch (start us, length us, event | category | flops | bytes accessed | tf_op | source)
XLA Modules:
  0.0 383.4 jit_solution(13826835870761128297)
XLA Ops:
  7.2 0.0 copy-start
  7.2 0.8 fusion.27
  8.0 0.1 copy.28
  8.1 0.1 reshape.207
  8.2 0.2 copy-done
  8.4 0.8 gather_fusion.1
  9.2 0.3 gather.10
  9.5 0.1 copy.27
  9.6 0.1 iota_compare_fusion
  9.7 0.0 copy-start.15
  9.7 0.0 copy-start.18
  9.7 0.0 copy-start.19
  9.7 0.0 copy-start.14
  9.7 0.0 copy-start.16
  9.7 1.9 broadcast_select_fusion
  11.7 4.5 %all-to-all-start = ((bf16[16,2,2,8192]{3,2,1,0:T(2,128)(2,1)}), bf16[16,2,2,8192]{3,2,1,0:T(2,128)(2,1)}, u32[]{:S(2)}, u32[]{:S(2)}) async-start(bf16[16,2,2,8192]{3,2,1,0:T(2,128)(2,1)} %broadcast_select_fusion), calls=%async_computation.1 | async-start | bytes 2097152 | tf_op jit(solution)/shard_map/all_to_all | solution.py:116
  16.1 0.0 reduce-scatter.2.cloned.1.call-start
  16.3 1.9 gather_fusion
  18.2 0.7 select_convert_fusion
  18.9 0.0 reduce-scatter.2.cloned.1.call-update
  19.0 0.0 all-reduce.4.cloned.1.call-start
  19.0 0.1 copy.31
  19.1 0.1 reshape_squeeze.3
  19.2 0.3 fusion.43
  19.6 1.2 copy.40
  20.7 0.4 convolution_convert_fusion.6
  21.1 1.9 reshape.197
  23.0 9.2 %all-to-all-done = bf16[16,2,2,8192]{3,2,1,0:T(2,128)(2,1)} async-done(((bf16[16,2,2,8192]{3,2,1,0:T(2,128)(2,1)}), bf16[16,2,2,8192]{3,2,1,0:T(2,128)(2,1)}, u32[]{:S(2)}, u32[]{:S(2)}) %all-to-all-start) | async-done | bytes 1048608 | tf_op jit(solution)/shard_map/all_to_all | solution.py:116
  32.2 3.4 copy.29
  35.6 2.7 reshape.196
  38.3 18.2 %reduce-scatter.2.cloned.1.call-done = bf16[32,128]{1,0:T(8,128)(2,1)} async-done(((bf16[256,128]{1,0:T(8,128)(2,1)}), bf16[32,128]{1,0:T(8,128)(2,1)}) %reduce-scatter.2.cloned.1.call-update) | async-done | bytes 8208 | tf_op jit(solution)/shard_map/reduce_scatter | solution.py:102
  56.5 2.1 fusion.13
  58.7 0.2 copy.30
  58.9 0.1 reshape_reshape.3
  59.1 0.3 fusion.41
  59.4 0.1 multiply_reduce_fusion.3
  59.5 3.1 convolution_convert_fusion
  62.7 5.3 %reshape.198 = bf16[32,16,3,8,48]{4,3,2,1,0:T(8,128)(2,1)} reshape(bf16[512,1152]{1,0:T(8,128)(2,1)} %convolution_convert_fusion) | data formatting | bytes 2359296 | tf_op jit(solution)/shard_map/reshape | solution.py:44
  67.9 3.7 fusion.40
  71.6 3.8 fusion.42
  75.4 2.3 convolution_convert_fusion.5
  77.8 1.9 fusion.5
  79.8 1.9 fusion.7
  81.7 0.0 copy-start.2
  81.7 2.5 fusion.8
  84.2 1.6 fusion.10
  85.9 0.5 fusion.9
  86.4 0.8 pad_maximum_fusion
  87.2 2.5 copy.39
  89.6 5.0 %reshape.199 = bf16[512,1152]{1,0:T(8,128)(2,1)} reshape(bf16[32,16,3,8,48]{4,3,2,1,0:T(8,128)(2,1)} %copy.39) | data formatting | bytes 2359296 | tf_op jit(solution)/shard_map/reshape | solution.py:57
  94.6 3.3 multiply_reduce_fusion.1
  98.0 1.9 fusion.37
  99.9 1.2 copy.41
  101.1 2.0 reshape.200
  103.2 1.2 fusion.22
  104.4 0.2 copy-done.10
  104.6 1.1 fusion.21
  105.7 0.0 all-reduce.4.cloned.1.call-update
  105.8 0.5 fusion.14
  106.3 74.6 %all-reduce = (f32[384]{0:T(512)}, f32[4,384]{1,0:T(4,128)}) all-reduce(f32[384]{0:T(512)S(1)} %get-tuple-element.5, f32[4,384]{1,0:T(4,128)S(1)} %fusion.14), channel_id=1, replica_groups=mesh['dp'=32,'frame'=8] {'dp','frame'}, use_global_device_ids=true, to_apply=%region_10.11 | all-reduce | flops 1920 | bytes 15360 | tf_op jit(solution)/shard_map/psum | solution.py:130
  180.9 190.4 %all-reduce.4.cloned.1.call-done = (f32[128,384]{1,0:T(8,128)}, f32[384,1152]{1,0:T(8,128)}, f32[384,384]{1,0:T(8,128)}) async-done(((f32[128,384]{1,0:T(8,128)}, f32[384,1152]{1,0:T(8,128)}, f32[384,384]{1,0:T(8,128)}), (f32[128,384]{1,0:T(8,128)}, f32[384,1152]{1,0:T(8,128)}, f32[384,384]{1,0:T(8,128)})) %all-reduce.4.cloned.1.call-update) | async-done | bytes 2555920 | tf_op jit(solution)/shard_map/psum | solution.py:130
  371.3 1.7 copy.85
  372.9 2.8 copy.86
  375.7 0.8 copy.87
  (38 shorter events, 0.2 us)
Async XLA Ops:
  7.2 1.2 copy-start
  8.4 1.1 copy-start.17
  9.7 6.5 %copy-start.15 = (s32[1,256]{1,0:T(1,128)S(1)}, s32[1,256]{1,0:T(1,128)}, u32[]{:S(2)}) copy-start(s32[1,256]{1,0:T(1,128)} %param.15) | copy-start | bytes 3076
  9.7 6.5 %copy-start.18 = (s32[1,256]{1,0:T(1,128)S(1)}, s32[1,256]{1,0:T(1,128)}, u32[]{:S(2)}) copy-start(s32[1,256]{1,0:T(1,128)} %param.17) | copy-start | bytes 3076
  9.7 6.5 %copy-start.19 = (s32[1,256]{1,0:T(1,128)S(1)}, s32[1,256]{1,0:T(1,128)}, u32[]{:S(2)}) copy-start(s32[1,256]{1,0:T(1,128)} %param.16) | copy-start | bytes 3076
  9.7 9.3 %copy-start.14 = (bf16[1,4,32,16]{2,3,1,0:T(8,128)(2,1)S(1)}, bf16[1,4,32,16]{2,3,1,0:T(8,128)(2,1)}, u32[]{:S(2)}) copy-start(bf16[1,4,32,16]{2,3,1,0:T(8,128)(2,1)} %param.18) | copy-start | bytes 12292
  9.7 9.5 %copy-start.16 = (bf16[4,384]{1,0:T(4,128)(2,1)S(1)}, bf16[4,384]{1,0:T(4,128)(2,1)}, u32[]{:S(2)}) copy-start(bf16[4,384]{1,0:T(4,128)(2,1)} %param.23) | copy-start | bytes 9220
  11.7 20.5 %all-to-all-start = ((bf16[16,2,2,8192]{3,2,1,0:T(2,128)(2,1)}), bf16[16,2,2,8192]{3,2,1,0:T(2,128)(2,1)}, u32[]{:S(2)}, u32[]{:S(2)}) async-start(bf16[16,2,2,8192]{3,2,1,0:T(2,128)(2,1)} %broadcast_select_fusion), calls=%async_computation.1 | async-start | bytes 2097152 | tf_op jit(solution)/shard_map/all_to_all | solution.py:116
  16.1 4.6 %copy-start.7 = (bf16[384,384]{1,0:T(8,128)(2,1)S(1)}, bf16[384,384]{1,0:T(8,128)(2,1)}, u32[]{:S(2)}) copy-start(bf16[384,384]{1,0:T(8,128)(2,1)} %param.22) | copy-start | bytes 884740
  16.1 40.4 %reduce-scatter.2.cloned.1.call-start = ((), (), s32[]{:S(2)}) async-start(), calls=%async_computation.2 | async-start | bytes 73728 | tf_op jit(solution)/shard_map/reduce_scatter | solution.py:102
  19.0 352.3 %all-reduce.4.cloned.1.call-start = ((), (), s32[]{:S(2)}) async-start(), calls=%async_computation.3 | async-start | bytes 5111808 | tf_op jit(solution)/shard_map/psum | solution.py:130
  35.6 23.4 %copy-start.12 = (bf16[128,384]{1,0:T(8,128)(2,1)S(1)}, bf16[128,384]{1,0:T(8,128)(2,1)}, u32[]{:S(2)}) copy-start(bf16[128,384]{1,0:T(8,128)(2,1)} %param.19) | copy-start | bytes 294916
  38.3 21.2 %copy-start.13 = (f32[384]{0:T(512)S(1)}, f32[384]{0:T(512)}, u32[]{:S(2)}) copy-start(f32[384]{0:T(512)} %param.20) | copy-start | bytes 4612
  75.4 2.4 copy-start.6
  77.8 1.9 copy-start.9
  79.7 1.9 copy-start.8
  81.7 2.5 copy-start.2
  84.2 1.7 copy-start.1
  94.6 3.3 copy-start.3
  98.0 1.9 copy-start.4
  103.2 1.2 copy-start.5
  103.2 1.5 copy-start.10
  371.3 4.5 %copy-start.11 = (f32[384,384]{1,0:T(8,128)S(1)}, f32[384,384]{1,0:T(8,128)}, u32[]{:S(2)}) copy-start(f32[384,384]{1,0:T(8,128)} %get-tuple-element.28) | copy-start | bytes 1769476
Sparse Core Ops, SparseCore 0:
  20.0 36.4 reduce-scatter.1
  105.9 265.3 all-reduce.3
where the time goes:
time: 384 us; the launch traced here: 383 us
  waiting for transfers between devices  218 us (57%)
  blocking collectives  74.6 us (19%)
  local copies, waits for them, and re-layouts  38.5 us (10%)
  matrix products  27.1 us (7%)
  between operations  14.4 us (4%)
  other arithmetic  6.41 us (2%)
  starting transfers between devices  4.55 us (1%)
    psum x1, waiting for transfers between devices, body(): lax.psum((g_in, g_gain, g_qkv, g_out, g_head), ('dp', 'frame'))  190 us
    psum x1, blocking collectives, body(): lax.psum((g_in, g_gain, g_qkv, g_out, g_head), ('dp', 'frame'))  74.6 us
    reduce_scatter x1, waiting for transfers between devices, body(): lax.psum_scatter(jnp.where(inside[:, None], picked, 0.0).astype(jnp.bfloa...  18.2 us
    all_to_all x1, waiting for transfers between devices, body(): lax.all_to_all(outgoing, 'frame', split_axis=0, concat_axis=1, tiled=True)  9.2 us
  transfers between devices with their start and end apart: 3, of which 3 were waited for; matrix products, arithmetic and copies ran while one was open for 3% of the time, Pallas kernels for 0%

commit v1 on v0

--- a/solution.py
+++ b/solution.py
@@ -4,6 +4,11 @@
 from jax.sharding import PartitionSpec as P
 
 HEADS = 8
+
+
+def load_modes_now(tile_in, axis_id, a_name):
+    oldest = lax.psum(tile_in, axis_id)
+    return lax.psum(oldest, a_name)
 
 
 def attend(query, keys, values):
@@ -127,8 +132,8 @@
     g_in, g_gain, g_qkv, g_out, g_head = local_grads(
         corr, cotangent[0], w_in, gain, w_qkv, w_out, w_head
     )
-    s_in, s_gain, s_qkv, s_out, s_head = lax.psum(
-        (g_in, g_gain, g_qkv, g_out, g_head), ("dp", "frame")
+    s_in, s_gain, s_qkv, s_out, s_head = load_modes_now(
+        (g_in, g_gain, g_qkv, g_out, g_head), "frame", "dp"
     )
     return (s_in, s_gain, s_qkv, s_out, s_head)
 

time: 384 us -> 349 us (0.909)
  waiting for transfers between devices: 218 us -> 178 us
  blocking collectives: 74.6 us -> 79.2 us
    psum x1 -> x2, waiting for transfers between devices: 190 us -> 150 us  [the longest x1 79.1 us: load_modes_now(): return lax.psum(oldest, a_name)]
    psum x1 -> x2, blocking collectives: 74.6 us -> 79.2 us  [the longest x1 65 us: load_modes_now(): return lax.psum(oldest, a_name)]
  transfers between devices with their start and end apart: 3 -> 4, of which waited for: 3 -> 4; matrix products, arithmetic and copies ran while one was open for 3% -> 4% of each run, Pallas kernels for 0% -> 0%
where the time goes in v1:
time: 349 us; the launch traced here: 348 us
  waiting for transfers between devices  178 us (51%)
  blocking collectives  79.2 us (23%)
  local copies, waits for them, and re-layouts  38.5 us (11%)
  matrix products  27.1 us (8%)
  between operations  14.1 us (4%)
  other arithmetic  6.41 us (2%)
  starting transfers between devices  4.59 us (1%)
    psum x1, waiting for transfers between devices, load_modes_now(): return lax.psum(oldest, a_name)  79.1 us
    psum x1, waiting for transfers between devices, load_modes_now(): oldest = lax.psum(tile_in, axis_id)  71.3 us
    psum x1, blocking collectives, load_modes_now(): return lax.psum(oldest, a_name)  65 us
    reduce_scatter x1, waiting for transfers between devices, body(): lax.psum_scatter(jnp.where(inside[:, None], picked, 0.0).astype(jnp.bfloa...  18.2 us
    psum x1, blocking collectives, load_modes_now(): oldest = lax.psum(tile_in, axis_id)  14.2 us
    all_to_all x1, waiting for transfers between devices, body(): lax.all_to_all(outgoing, 'frame', split_axis=0, concat_axis=1, tiled=True)  9.2 us
  transfers between devices with their start and end apart: 4, of which 4 were waited for; matrix products, arithmetic and copies ran while one was open for 4% of the time, Pallas kernels for 0%

profile of v1, /device:TPU:2, one launch (start us, length us, event | category | flops | bytes accessed | tf_op | source)
XLA Modules:
  0.0 347.8 jit_solution(14156932568979104859)
XLA Ops:
  7.2 0.0 copy-start
  7.2 0.8 fusion.27
  8.0 0.1 copy.28
  8.1 0.1 reshape.207
  8.2 0.2 copy-done
  8.4 0.8 gather_fusion.1
  9.2 0.3 gather.10
  9.5 0.1 copy.27
  9.6 0.1 iota_compare_fusion
  9.7 0.0 copy-start.18
  9.7 0.0 copy-start.19
  9.7 1.9 broadcast_select_fusion
  11.7 4.5 %all-to-all-start = ((bf16[16,2,2,8192]{3,2,1,0:T(2,128)(2,1)}), bf16[16,2,2,8192]{3,2,1,0:T(2,128)(2,1)}, u32[]{:S(2)}, u32[]{:S(2)}) async-start(bf16[16,2,2,8192]{3,2,1,0:T(2,128)(2,1)} %broadcast_select_fusion), calls=%async_computation.1 | async-start | bytes 2097152 | tf_op jit(solution)/shard_map/all_to_all | solution.py:121
  16.1 0.0 reduce-scatter.2.cloned.1.call-start
  16.3 1.9 gather_fusion
  18.2 0.7 select_convert_fusion
  18.9 0.0 reduce-scatter.2.cloned.1.call-update
  19.0 0.0 all-reduce.9.cloned.1.call-start
  19.0 0.1 copy.31
  19.1 0.1 reshape_squeeze.3
  19.2 0.3 fusion.43
  19.6 1.2 copy.40
  20.7 0.4 convolution_convert_fusion.6
  21.1 1.9 reshape.197
  23.0 9.2 %all-to-all-done = bf16[16,2,2,8192]{3,2,1,0:T(2,128)(2,1)} async-done(((bf16[16,2,2,8192]{3,2,1,0:T(2,128)(2,1)}), bf16[16,2,2,8192]{3,2,1,0:T(2,128)(2,1)}, u32[]{:S(2)}, u32[]{:S(2)}) %all-to-all-start) | async-done | bytes 1048608 | tf_op jit(solution)/shard_map/all_to_all | solution.py:121
  32.2 3.4 copy.29
  35.6 2.7 reshape.196
  38.3 18.2 %reduce-scatter.2.cloned.1.call-done = bf16[32,128]{1,0:T(8,128)(2,1)} async-done(((bf16[256,128]{1,0:T(8,128)(2,1)}), bf16[32,128]{1,0:T(8,128)(2,1)}) %reduce-scatter.2.cloned.1.call-update) | async-done | bytes 8208 | tf_op jit(solution)/shard_map/reduce_scatter | solution.py:107
  56.5 2.1 fusion.13
  58.7 0.2 copy.30
  58.9 0.1 reshape_reshape.3
  59.1 0.3 fusion.41
  59.4 0.1 multiply_reduce_fusion.3
  59.5 3.1 convolution_convert_fusion
  62.7 5.3 %reshape.198 = bf16[32,16,3,8,48]{4,3,2,1,0:T(8,128)(2,1)} reshape(bf16[512,1152]{1,0:T(8,128)(2,1)} %convolution_convert_fusion) | data formatting | bytes 2359296 | tf_op jit(solution)/shard_map/reshape | solution.py:49
  67.9 3.7 %fusion.40 = (bf16[32,16,1,8,48]{4,3,2,1,0:T(8,128)(2,1)}, bf16[32,16,1,8,48]{4,3,2,1,0:T(8,128)(2,1)}, bf16[32,16,1,8,48]{4,3,2,1,0:T(8,128)(2,1)}) fusion(bf16[32,16,3,8,48]{4,3,2,1,0:T(8,128)(2,1)} %reshape.198), kind=kLoop, calls=%fused_computation.78 | loop fusion | bytes 2359296 | tf_op jit(solution)/shard_map/slice | solution.py:50
  71.6 3.8 %fusion.42 = (f32[32,8,16]{2,1,0:T(8,128)S(1)}, f32[32,8,16,16]{3,2,1,0:T(8,128)}) fusion(bf16[32,16,1,8,48]{4,3,2,1,0:T(8,128)(2,1)} %get-tuple-element.20, bf16[32,16,1,8,48]{4,3,2,1,0:T(8,128)(2,1)} %get-tuple-element.19), kind=kOutput, calls=%fused_computation.80 | convolution fusion | flops 6488079 | bytes 1064960 | tf_op jit(solution)/shard_map/jvp()/sub | solution.py:19
  75.4 2.3 convolution_convert_fusion.5
  77.8 1.9 fusion.5
  79.8 1.9 fusion.7
  81.7 2.5 fusion.8
  84.2 1.6 fusion.10
  85.9 0.5 fusion.9
  86.4 0.8 pad_maximum_fusion
  87.2 2.5 copy.39
  89.6 5.0 %reshape.199 = bf16[512,1152]{1,0:T(8,128)(2,1)} reshape(bf16[32,16,3,8,48]{4,3,2,1,0:T(8,128)(2,1)} %copy.39) | data formatting | bytes 2359296 | tf_op jit(solution)/shard_map/reshape | solution.py:62
  94.6 3.3 multiply_reduce_fusion.1
  98.0 1.9 fusion.37
  99.9 1.2 copy.41
  101.1 2.0 reshape.200
  103.2 1.2 fusion.22
  104.4 0.2 copy-done.10
  104.6 1.1 fusion.21
  105.7 0.0 all-reduce.9.cloned.1.call-update
  105.8 0.0 all-reduce.7.cloned.1.call-start
  105.8 71.3 %all-reduce.9.cloned.1.call-done = (f32[128,384]{1,0:T(8,128)}, f32[384,1152]{1,0:T(8,128)}, f32[384,384]{1,0:T(8,128)}) async-done(((f32[128,384]{1,0:T(8,128)}, f32[384,1152]{1,0:T(8,128)}, f32[384,384]{1,0:T(8,128)}), (f32[128,384]{1,0:T(8,128)}, f32[384,1152]{1,0:T(8,128)}, f32[384,384]{1,0:T(8,128)})) %all-reduce.9.cloned.1.call-update) | async-done | bytes 2555920 | tf_op jit(solution)/shard_map/psum | solution.py:10
  177.1 0.0 all-reduce.7.cloned.1.call-update
  177.1 0.5 fusion.14
  177.7 14.2 %all-reduce.2 = (f32[384]{0:T(512)S(1)}, f32[4,384]{1,0:T(4,128)S(1)}) all-reduce(f32[384]{0:T(512)S(1)} %get-tuple-element.5, f32[4,384]{1,0:T(4,128)S(1)} %fusion.14), channel_id=1, replica_groups=mesh['dp'=32,'frame'=8] {'frame'}, use_global_device_ids=true, to_apply=%region_11.12 | all-reduce | flops 1920 | bytes 15360 | tf_op jit(solution)/shard_map/psum | solution.py:10
  191.8 65.0 %all-reduce = (f32[384]{0:T(512)}, f32[4,384]{1,0:T(4,128)}) all-reduce(f32[384]{0:T(512)S(1)} %get-tuple-element.13, f32[4,384]{1,0:T(4,128)S(1)} %get-tuple-element.14), channel_id=1, replica_groups=mesh['dp'=32,'frame'=8] {'dp'}, use_global_device_ids=true, to_apply=%region_12.13 | all-reduce | flops 1920 | bytes 15360 | tf_op jit(solution)/shard_map/psum | solution.py:11
  256.9 79.1 %all-reduce.7.cloned.1.call-done = (f32[128,384]{1,0:T(8,128)}, f32[384,1152]{1,0:T(8,128)}, f32[384,384]{1,0:T(8,128)}) async-done(((f32[128,384]{1,0:T(8,128)}, f32[384,1152]{1,0:T(8,128)}, f32[384,384]{1,0:T(8,128)}), (f32[128,384]{1,0:T(8,128)}, f32[384,1152]{1,0:T(8,128)}, f32[384,384]{1,0:T(8,128)})) %all-reduce.7.cloned.1.call-update) | async-done | bytes 2555920 | tf_op jit(solution)/shard_map/psum | solution.py:11
  336.0 1.7 copy.88
  337.7 2.8 copy.89
  340.5 0.8 copy.90
  (42 shorter events, 0.2 us)
Async XLA Ops:
  7.2 1.2 copy-start
  8.4 1.1 copy-start.17
  9.7 6.5 %copy-start.15 = (s32[1,256]{1,0:T(1,128)S(1)}, s32[1,256]{1,0:T(1,128)}, u32[]{:S(2)}) copy-start(s32[1,256]{1,0:T(1,128)} %param.15) | copy-start | bytes 3076
  9.7 6.5 %copy-start.18 = (s32[1,256]{1,0:T(1,128)S(1)}, s32[1,256]{1,0:T(1,128)}, u32[]{:S(2)}) copy-start(s32[1,256]{1,0:T(1,128)} %param.17) | copy-start | bytes 3076
  9.7 6.5 %copy-start.19 = (s32[1,256]{1,0:T(1,128)S(1)}, s32[1,256]{1,0:T(1,128)}, u32[]{:S(2)}) copy-start(s32[1,256]{1,0:T(1,128)} %param.16) | copy-start | bytes 3076
  9.7 9.3 %copy-start.14 = (bf16[1,4,32,16]{2,3,1,0:T(8,128)(2,1)S(1)}, bf16[1,4,32,16]{2,3,1,0:T(8,128)(2,1)}, u32[]{:S(2)}) copy-start(bf16[1,4,32,16]{2,3,1,0:T(8,128)(2,1)} %param.18) | copy-start | bytes 12292
  9.7 9.5 %copy-start.16 = (bf16[4,384]{1,0:T(4,128)(2,1)S(1)}, bf16[4,384]{1,0:T(4,128)(2,1)}, u32[]{:S(2)}) copy-start(bf16[4,384]{1,0:T(4,128)(2,1)} %param.23) | copy-start | bytes 9220
  11.7 20.5 %all-to-all-start = ((bf16[16,2,2,8192]{3,2,1,0:T(2,128)(2,1)}), bf16[16,2,2,8192]{3,2,1,0:T(2,128)(2,1)}, u32[]{:S(2)}, u32[]{:S(2)}) async-start(bf16[16,2,2,8192]{3,2,1,0:T(2,128)(2,1)} %broadcast_select_fusion), calls=%async_computation.1 | async-start | bytes 2097152 | tf_op jit(solution)/shard_map/all_to_all | solution.py:121
  16.1 4.6 %copy-start.7 = (bf16[384,384]{1,0:T(8,128)(2,1)S(1)}, bf16[384,384]{1,0:T(8,128)(2,1)}, u32[]{:S(2)}) copy-start(bf16[384,384]{1,0:T(8,128)(2,1)} %param.22) | copy-start | bytes 884740
  16.1 40.4 %reduce-scatter.2.cloned.1.call-start = ((), (), s32[]{:S(2)}) async-start(), calls=%async_computation.2 | async-start | bytes 73728 | tf_op jit(solution)/shard_map/reduce_scatter | solution.py:107
  19.0 158.1 %all-reduce.9.cloned.1.call-start = ((), (), s32[]{:S(2)}) async-start(), calls=%async_computation.4 | async-start | bytes 5111808 | tf_op jit(solution)/shard_map/psum | solution.py:10
  35.6 23.4 %copy-start.12 = (bf16[128,384]{1,0:T(8,128)(2,1)S(1)}, bf16[128,384]{1,0:T(8,128)(2,1)}, u32[]{:S(2)}) copy-start(bf16[128,384]{1,0:T(8,128)(2,1)} %param.19) | copy-start | bytes 294916
  38.3 21.2 %copy-start.13 = (f32[384]{0:T(512)S(1)}, f32[384]{0:T(512)}, u32[]{:S(2)}) copy-start(f32[384]{0:T(512)} %param.20) | copy-start | bytes 4612
  75.4 2.4 copy-start.6
  77.8 1.9 copy-start.9
  79.7 1.9 copy-start.8
  81.7 2.5 copy-start.2
  84.2 1.7 copy-start.1
  94.6 3.3 copy-start.3
  98.0 1.9 copy-start.4
  103.2 1.2 copy-start.5
  103.2 1.5 copy-start.10
  105.8 230.3 %all-reduce.7.cloned.1.call-start = ((), (), s32[]{:S(2)}) async-start(), calls=%async_computation.3 | async-start | bytes 5111808 | tf_op jit(solution)/shard_map/psum | solution.py:11
  336.0 4.5 %copy-start.11 = (f32[384,384]{1,0:T(8,128)S(1)}, f32[384,384]{1,0:T(8,128)}, u32[]{:S(2)}) copy-start(f32[384,384]{1,0:T(8,128)} %get-tuple-element.33) | copy-start | bytes 1769476
Sparse Core Ops, SparseCore 0:
  20.0 36.4 reduce-scatter.1
  105.9 71.1 all-reduce.8
  180.9 155.0 all-reduce.6
